TPU v7x, 256 devices: a whole 4x4x8 slice. The times are simulated.
256 devices in a mesh: region: 32 (over y, z), sub: 8 (over x, core).
Axes of the slice: x: 4, y: 4, z: 8, core: 2. Of those that a mesh axis runs over, the one named last changes fastest.
Arguments:
- mode_rows: bfloat16 [131072, 4096], P(('region', 'sub')), may hold values from -0.09375 to 0.09375
- input_rows: bfloat16 [512, 4096], P(('region', 'sub')), may hold values from -0.25 to 0.25
- input_factor: bfloat16 [512, 128], P(('region', 'sub')), may hold values from -6 to 6
- mode_freq: float32 [4096], replicated, may hold values from 0.5 to 2
- mode_damping: float32 [4096], replicated, may hold values from 0.02 to 0.2
- line_freq: float32 [2], replicated, may hold values from 0.6 to 1.6
- boundary_rows: int32 [32768], P(('region', 'sub')), may hold values from 0 to 511
- connectivity: int32 [4, 131072], P(None, ('region', 'sub')), may hold values from 0 to 639
- stress_coef: float32 [4, 131072], P(None, ('region', 'sub')), may hold values from -3 to 3
Outputs:
- stress_psd: float32 [2, 131072], P(None, ('region', 'sub'))
Inputs may be any that keep to these rules, and one draw needn't show every extreme that they name: `boundary_rows`: local row numbers of the sending device. `connectivity`: rows of the node table of the element's device.
All inputs are finite; a program needn't handle non-finite values.
Results may differ from a plain program's by a relative error of at most 0.0013.
Values may be sent and summed in bfloat16 or wider, within the bound.
A program may use at most 64 MiB of HBM per device.

v0:
```python
import jax
import jax.numpy as jnp
from jax import lax
from jax.sharding import PartitionSpec as P


def extended(cells, sides, width):
    for axis, dim in sides:
        count = lax.axis_size(axis)
        ends = count - 1
        head = lax.slice_in_dim(cells, 0, width, axis=dim)
        tail = lax.slice_in_dim(cells, cells.shape[dim] - width, cells.shape[dim], axis=dim)
        cells = jnp.concatenate(
            [
                lax.ppermute(tail, axis, [(i, (i + 1) % count) for i in range(ends)]),
                cells,
                lax.ppermute(head, axis, [((i + 1) % count, i) for i in range(ends)]),
            ],
            axis=dim,
        )
    return cells


def modal_gain(mode_freq, mode_damping, line_omega):
    detune = mode_freq * mode_freq - line_omega * line_omega
    damped = 2.0 * mode_damping * mode_freq * line_omega
    magnitude = detune * detune + damped * damped
    return (detune / magnitude, -damped / magnitude)


def apply_gain(summed, gain_real, gain_imag):
    half_cols = summed.shape[1] // 2
    forced_real = summed[:, :half_cols]
    forced_imag = summed[:, half_cols:]
    out_real = gain_real[:, None] * forced_real - gain_imag[:, None] * forced_imag
    out_imag = gain_real[:, None] * forced_imag + gain_imag[:, None] * forced_real
    return jnp.concatenate([out_real, out_imag], axis=1).astype(jnp.bfloat16)


def scale_lines(summed, mode_freq, mode_damping, line_freq, columns):
    pieces = []
    for line_no in range(line_freq.shape[0]):
        gain_real, gain_imag = modal_gain(mode_freq, mode_damping, line_freq[line_no])
        pieces.append(
            apply_gain(summed[:, line_no * columns : (line_no + 1) * columns], gain_real, gain_imag)
        )
    return jnp.concatenate(pieces, axis=1)


def local(
    mode_rows,
    input_rows,
    input_factor,
    mode_freq,
    mode_damping,
    line_freq,
    boundary_rows,
    connectivity,
    stress_coef,
):
    mode_count = input_rows.shape[1]
    line_count = line_freq.shape[0]
    width_all = input_factor.shape[1]
    columns = width_all // line_count
    partial_value = lax.dot_general(
        input_rows, input_factor, (((0,), (0,)), ((), ())), preferred_element_type=jnp.float32
    )
    summed = lax.psum(
        partial_value.reshape(mode_count // 2, 2 * width_all), ("region", "sub")
    ).reshape(mode_count, width_all)
    pseudo = scale_lines(summed, mode_freq, mode_damping, line_freq, columns)
    responses = jnp.dot(mode_rows, pseudo, preferred_element_type=jnp.float32).astype(jnp.bfloat16)
    rim_rows = boundary_rows.shape[0] // 2
    export = responses[boundary_rows]
    padded = extended(export, ((("region", "sub"), 0),), rim_rows)
    node_table = jnp.concatenate([padded[:rim_rows], responses, padded[3 * rim_rows :]], axis=0)
    stress = stress_coef[0][:, None] * node_table[connectivity[0]].astype(jnp.float32)
    for corner in range(1, connectivity.shape[0]):
        stress = stress + stress_coef[corner][:, None] * node_table[connectivity[corner]].astype(
            jnp.float32
        )
    squares = stress * stress
    power = jnp.stack(
        [
            jnp.mean(squares[:, line_no * columns : (line_no + 1) * columns], axis=1)
            for line_no in range(line_count)
        ],
        axis=0,
    )
    return power


def solution(mesh):
    placed = (
        P(("region", "sub"), None),
        P(("region", "sub"), None),
        P(("region", "sub"), None),
        P(),
        P(),
        P(),
        P(("region", "sub")),
        P(None, ("region", "sub")),
        P(None, ("region", "sub")),
    )
    return jax.shard_map(
        local, mesh=mesh, in_specs=placed, out_specs=P(None, ("region", "sub")), check_vma=False
    )
```

profile of v0, /device:TPU:24, one launch (start us, length us, event | category | flops | bytes accessed | tf_op | source)
XLA Modules:
  0.0 312.2 jit_solution(9872141562445316333)
XLA Ops:
  6.6 0.0 all-reduce.2.cloned.1.call-start
  6.6 0.6 copy-done
  7.3 2.4 fusion.14
  9.7 0.6 fusion.13
  12.9 1.2 fusion.9
  14.2 262.5 %all-reduce.2.cloned.1.call-done = f32[4096,128]{0,1:T(8,128)} async-done(((f32[4096,128]{0,1:T(8,128)}), f32[4096,128]{0,1:T(8,128)}) %all-reduce.2.cloned.1.call-update) | async-done | bytes 2097168 | tf_op jit(solution)/shard_map/psum | solution.py:68
  276.7 1.8 subtract_convert_fusion.1
  278.5 3.7 %fusion = bf16[512,128]{0,1:T(8,128)(2,1)S(1)} fusion(bf16[512,4096]{1,0:T(8,128)(2,1)} %param.9, bf16[4096,32]{0,1:T(8,128)(2,1)S(1)} %get-tuple-element.11, bf16[4096,32]{0,1:T(8,128)(2,1)S(1)} %get-tuple-element.12, bf16[4096,32]{0,1:T(8,128)(2,1)S(1)} %get-tuple-element.8, bf16[4096,32]{0,1:T(8,128)(2,1)S(1)} %get-tuple-element.7), kind=kOutput, calls=%fused_computation.6 | convolution fusion | flops 541130752 | bytes 5373952 | tf_op jit(solution)/shard_map/dot_general | solution.py:72
  282.2 0.1 copy.25
  282.3 0.7 gather_fusion
  283.0 0.1 copy.34
  283.1 5.7 %collective-permute-start.1 = (bf16[64,128]{0,1:T(8,128)(2,1)S(1)}, bf16[64,128]{0,1:T(8,128)(2,1)S(1)}, u32[]{:S(2)}, u32[]{:S(2)}) collective-permute-start(bf16[64,128]{0,1:T(8,128)(2,1)S(1)} %copy.34), channel_id=1, source_target_pairs={{1,0},{2,1},{3,2},{4,3},{5,4},{6,5},{7,6},{8,7},{9,8},{10,9},{11,1... | collective-permute-start | bytes 49160 | tf_op jit(solution)/shard_map/ppermute | solution.py:17
  288.8 0.1 copy.33
  289.0 1.9 collective-permute-start
  290.9 7.5 %collective-permute-done = bf16[64,128]{0,1:T(8,128)(2,1)S(1)} collective-permute-done((bf16[64,128]{0,1:T(8,128)(2,1)S(1)}, bf16[64,128]{0,1:T(8,128)(2,1)S(1)}, u32[]{:S(2)}, u32[]{:S(2)}) %collective-permute-start) | collective-permute-done | bytes 16416 | tf_op jit(solution)/shard_map/ppermute | solution.py:15
  298.4 0.1 pad_maximum_fusion
  298.5 0.2 copy.28
  298.7 1.3 gather_fusion.4
  300.1 1.3 gather_fusion.3
  301.4 1.3 gather_fusion.2
  302.7 1.3 gather_fusion.1
  304.1 0.3 add_multiply_fusion
  304.4 0.3 slice_reduce_fusion.1
  304.8 0.6 pad_maximum_fusion.1
  (25 shorter events, 0.1 us)
Async XLA Ops:
  6.5 0.7 copy-start
  6.5 3.2 %copy-start.5 = (f32[2]{0:T(128)S(1)}, f32[2]{0:T(128)}, u32[]{:S(2)}) copy-start(f32[2]{0:T(128)} %param.14) | copy-start | bytes 28
  6.5 3.8 %copy-start.6 = (s32[128]{0:T(128)S(1)}, s32[128]{0:T(128)}, u32[]{:S(2)}) copy-start(s32[128]{0:T(128)} %param.15) | copy-start | bytes 1540
  6.5 6.2 %copy-start.3 = (s32[4,512]{1,0:T(4,128)S(1)}, s32[4,512]{1,0:T(4,128)}, u32[]{:S(2)}) copy-start(s32[4,512]{1,0:T(4,128)} %param.16) | copy-start | bytes 24580
  6.5 6.3 %copy-start.4 = (f32[4,512]{1,0:T(4,128)S(1)}, f32[4,512]{1,0:T(4,128)}, u32[]{:S(2)}) copy-start(f32[4,512]{1,0:T(4,128)} %param.17) | copy-start | bytes 24580
  6.5 6.3 %copy-start.1 = (f32[4096]{0:T(1024)S(1)}, f32[4096]{0:T(1024)}, u32[]{:S(2)}) copy-start(f32[4096]{0:T(1024)} %param.12) | copy-start | bytes 49156
  6.6 6.3 %copy-start.2 = (f32[4096]{0:T(1024)S(1)}, f32[4096]{0:T(1024)}, u32[]{:S(2)}) copy-start(f32[4096]{0:T(1024)} %param.13) | copy-start | bytes 49156
  6.6 270.1 %all-reduce.2.cloned.1.call-start = ((), (), s32[]{:S(2)}) async-start(), calls=%async_computation | async-start | bytes 4194304 | tf_op jit(solution)/shard_map/psum | solution.py:68
  283.1 7.8 %collective-permute-start.1 = (bf16[64,128]{0,1:T(8,128)(2,1)S(1)}, bf16[64,128]{0,1:T(8,128)(2,1)S(1)}, u32[]{:S(2)}, u32[]{:S(2)}) collective-permute-start(bf16[64,128]{0,1:T(8,128)(2,1)S(1)} %copy.34), channel_id=1, source_target_pairs={{1,0},{2,1},{3,2},{4,3},{5,4},{6,5},{7,6},{8,7},{9,8},{10,9},{11,1... | collective-permute-start | bytes 49160 | tf_op jit(solution)/shard_map/ppermute | solution.py:17
  289.0 9.5 %collective-permute-start = (bf16[64,128]{0,1:T(8,128)(2,1)S(1)}, bf16[64,128]{0,1:T(8,128)(2,1)S(1)}, u32[]{:S(2)}, u32[]{:S(2)}) collective-permute-start(bf16[64,128]{0,1:T(8,128)(2,1)S(1)} %copy.33), channel_id=1, source_target_pairs={{0,1},{1,2},{2,3},{3,4},{4,5},{5,6},{6,7},{7,8},{8,9},{9,10},{10,1... | collective-permute-start | bytes 49160 | tf_op jit(solution)/shard_map/ppermute | solution.py:15
Sparse Core Ops, SparseCore 0:
  12.8 263.8 all-reduce.1
where the time goes:
time: 313 us; the launch traced here: 312 us
  waiting for transfers between devices  270 us (86%)
  between operations  16.1 us (5%)
  local copies, waits for them, and re-layouts  7.86 us (3%)
  starting transfers between devices  7.65 us (2%)
  matrix products  6.16 us (2%)
  other arithmetic  4.44 us (1%)
    psum x1, waiting for transfers between devices, local(): lax.psum(partial_value.reshape(mode_count // 2, 2 * width_all), ('region'...  263 us
    ppermute x1, waiting for transfers between devices, extended(): lax.ppermute(tail, axis, [(i, (i + 1) % count) for i in range(ends)])  7.5 us
  transfers between devices with their start and end apart: 3, of which 2 were waited for; matrix products, arithmetic and copies ran while one was open for 1% of the time, Pallas kernels for 0%

commit v1 on v0

--- a/solution.py
+++ b/solution.py
@@ -66,7 +66,7 @@
         input_rows, input_factor, (((0,), (0,)), ((), ())), preferred_element_type=jnp.float32
     )
     summed = lax.psum(
-        partial_value.reshape(mode_count // 2, 2 * width_all), ("region", "sub")
+        lax.psum(partial_value.reshape(mode_count // 2, 2 * width_all), "sub"), "region"
     ).reshape(mode_count, width_all)
     pseudo = scale_lines(summed, mode_freq, mode_damping, line_freq, columns)
     responses = jnp.dot(mode_rows, pseudo, preferred_element_type=jnp.float32).astype(jnp.bfloat16)

time: 313 us -> 272 us (0.87)
  waiting for transfers between devices: 270 us -> 228 us
  local copies, waits for them, and re-layouts: 7.86 us -> 13.7 us
  starting transfers between devices: 7.65 us -> 4.37 us
    psum x1 -> x2, waiting for transfers between devices: 263 us -> 221 us  [the longest x1 147 us: local(): lax.psum(lax.psum(partial_value.reshape(mode_count // 2, 2 * width_all),...]
    reshape x0 -> x3, local copies, waits for them, and re-layouts: none -> 5.12 us  [the longest x2 3.49 us: local(): summed = lax.psum(lax.psum(partial_value.reshape(mode_count // 2, 2 * wid...]
    ppermute x1, starting transfers between devices: 5.69 us -> 2.29 us  [extended(): lax.ppermute(head, axis, [((i + 1) % count, i) for i in range(ends)])]
  transfers between devices with their start and end apart: 3 -> 4, of which waited for: 2 -> 3; matrix products, arithmetic and copies ran while one was open for 1% -> 1% of each run, Pallas kernels for 0% -> 0%
where the time goes in v1:
time: 272 us; the launch traced here: 271 us
  waiting for transfers between devices  228 us (84%)
  between operations  16.1 us (6%)
  local copies, waits for them, and re-layouts  13.7 us (5%)
  matrix products  4.9 us (2%)
  other arithmetic  4.43 us (2%)
  starting transfers between devices  4.37 us (2%)
    psum x1, waiting for transfers between devices, local(): lax.psum(lax.psum(partial_value.reshape(mode_count // 2, 2 * width_all),...  147 us
    psum x1, waiting for transfers between devices, local(): lax.psum(partial_value.reshape(mode_count // 2, 2 * width_all), 'sub')  73.6 us
    ppermute x1, waiting for transfers between devices, extended(): lax.ppermute(tail, axis, [(i, (i + 1) % count) for i in range(ends)])  7.38 us
  transfers between devices with their start and end apart: 4, of which 3 were waited for; matrix products, arithmetic and copies ran while one was open for 1% of the time, Pallas kernels for 0%

profile of v1, /device:TPU:24, one launch (start us, length us, event | category | flops | bytes accessed | tf_op | source)
XLA Modules:
  0.0 271.4 jit_solution(16166180158244890134)
XLA Ops:
  6.5 0.7 copy-done
  7.3 1.2 fusion.14
  8.4 1.6 reshape.144
  10.1 73.6 %all-reduce.3.cloned.1.call-done = f32[2048,256]{1,0:T(8,128)} async-done(((f32[2048,256]{1,0:T(8,128)}), f32[2048,256]{1,0:T(8,128)}) %all-reduce.3.cloned.1.call-update) | async-done | bytes 2097168 | tf_op jit(solution)/shard_map/psum | solution.py:69
  83.7 1.6 reshape.145
  85.4 1.9 copy.31
  87.3 0.6 copy-done.5
  87.9 0.6 fusion.13
  91.1 1.2 fusion.9
  92.3 147.0 %all-reduce.5.cloned.1.call-done = f32[4096,128]{0,1:T(8,128)} async-done(((f32[4096,128]{0,1:T(8,128)}), f32[4096,128]{0,1:T(8,128)}) %all-reduce.5.cloned.1.call-update) | async-done | bytes 2097168 | tf_op jit(solution)/shard_map/psum | solution.py:68
  239.3 1.8 subtract_convert_fusion.1
  241.1 3.7 %fusion = bf16[512,128]{0,1:T(8,128)(2,1)S(1)} fusion(bf16[512,4096]{1,0:T(8,128)(2,1)} %param.9, bf16[4096,32]{0,1:T(8,128)(2,1)S(1)} %get-tuple-element.11, bf16[4096,32]{0,1:T(8,128)(2,1)S(1)} %get-tuple-element.12, bf16[4096,32]{0,1:T(8,128)(2,1)S(1)} %get-tuple-element.8, bf16[4096,32]{0,1:T(8,128)(2,1)S(1)} %get-tuple-element.7), kind=kOutput, calls=%fused_computation.6 | convolution fusion | flops 541130752 | bytes 5373952 | tf_op jit(solution)/shard_map/dot_general | solution.py:72
  244.9 0.7 gather_fusion
  245.8 2.3 collective-permute-start.1
  248.2 2.0 collective-permute-start
  250.3 7.4 %collective-permute-done = bf16[64,128]{0,1:T(8,128)(2,1)S(1)} collective-permute-done((bf16[64,128]{0,1:T(8,128)(2,1)S(1)}, bf16[64,128]{0,1:T(8,128)(2,1)S(1)}, u32[]{:S(2)}, u32[]{:S(2)}) %collective-permute-start) | collective-permute-done | bytes 16416 | tf_op jit(solution)/shard_map/ppermute | solution.py:15
  257.8 0.2 copy.35
  257.9 1.3 gather_fusion.4
  259.3 1.3 gather_fusion.3
  260.6 1.3 gather_fusion.2
  262.0 1.3 gather_fusion.1
  263.3 0.3 add_multiply_fusion
  263.7 0.3 slice_reduce_fusion.1
  264.0 0.6 pad_maximum_fusion.1
  (31 shorter events, 0.6 us)
Async XLA Ops:
  6.5 0.7 copy-start
  6.5 77.2 %all-reduce.3.cloned.1.call-start = ((), (), s32[]{:S(2)}) async-start(), calls=%async_computation | async-start | bytes 4194304 | tf_op jit(solution)/shard_map/psum | solution.py:69
  10.1 229.2 %all-reduce.5.cloned.1.call-start = ((), (), s32[]{:S(2)}) async-start(), calls=%async_computation.1 | async-start | bytes 4194304 | tf_op jit(solution)/shard_map/psum | solution.py:68
  87.2 0.7 copy-start.5
  87.2 3.7 %copy-start.6 = (s32[128]{0:T(128)S(1)}, s32[128]{0:T(128)}, u32[]{:S(2)}) copy-start(s32[128]{0:T(128)} %param.15) | copy-start | bytes 1540
  87.2 3.7 %copy-start.3 = (s32[4,512]{1,0:T(4,128)S(1)}, s32[4,512]{1,0:T(4,128)}, u32[]{:S(2)}) copy-start(s32[4,512]{1,0:T(4,128)} %param.16) | copy-start | bytes 24580
  87.2 3.8 %copy-start.4 = (f32[4,512]{1,0:T(4,128)S(1)}, f32[4,512]{1,0:T(4,128)}, u32[]{:S(2)}) copy-start(f32[4,512]{1,0:T(4,128)} %param.17) | copy-start | bytes 24580
  87.2 3.8 %copy-start.1 = (f32[4096]{0:T(1024)S(1)}, f32[4096]{0:T(1024)}, u32[]{:S(2)}) copy-start(f32[4096]{0:T(1024)} %param.12) | copy-start | bytes 49156
  87.2 3.8 %copy-start.2 = (f32[4096]{0:T(1024)S(1)}, f32[4096]{0:T(1024)}, u32[]{:S(2)}) copy-start(f32[4096]{0:T(1024)} %param.13) | copy-start | bytes 49156
  245.8 4.5 %collective-permute-start.1 = (bf16[64,128]{0,1:T(8,128)(2,1)S(1)}, bf16[64,128]{0,1:T(8,128)(2,1)S(1)}, u32[]{:S(2)}, u32[]{:S(2)}) collective-permute-start(bf16[64,128]{0,1:T(8,128)(2,1)S(1)} %copy.40), channel_id=1, source_target_pairs={{1,0},{2,1},{3,2},{4,3},{5,4},{6,5},{7,6},{8,7},{9,8},{10,9},{11,1... | collective-permute-start | bytes 49160 | tf_op jit(solution)/shard_map/ppermute | solution.py:17
  248.2 9.5 %collective-permute-start = (bf16[64,128]{0,1:T(8,128)(2,1)S(1)}, bf16[64,128]{0,1:T(8,128)(2,1)S(1)}, u32[]{:S(2)}, u32[]{:S(2)}) collective-permute-start(bf16[64,128]{0,1:T(8,128)(2,1)S(1)} %copy.39), channel_id=1, source_target_pairs={{0,1},{1,2},{2,3},{3,4},{4,5},{5,6},{6,7},{7,8},{8,9},{9,10},{10,1... | collective-permute-start | bytes 49160 | tf_op jit(solution)/shard_map/ppermute | solution.py:15
Sparse Core Ops, SparseCore 0:
  10.2 73.4 all-reduce.2
  87.4 151.8 all-reduce.4
